TPU v7x, 32 devices: a whole 2x2x4 slice. The times are simulated.
32 devices in a mesh: ctx: 4 (over y, x), tp: 4 (over z), grp: 2 (over core).
Axes of the slice: x: 2, y: 2, z: 4, core: 2. Of those that a mesh axis runs over, the one named last changes fastest.
Arguments:
- patches: bfloat16 [32, 5120], P('ctx'), may hold values from -6 to 6
- route_count: int32 [4, 4], replicated, may hold values from 0 to 2, as said below
- text_states: bfloat16 [512, 4096], P('ctx', ('tp', 'grp')), may hold values from -6 to 6
- segment_ids: int32 [512], replicated, may hold values from 0 to 3, never falling along the last dimension, each value on 1 to 256 neighbouring positions
- vision_gain: float32 [1280], replicated, may hold values from 0.1 to 1.9
- merge_up: bfloat16 [5120, 2560], P(None, ('tp', 'grp')), may hold values from -0.078125 to 0.078125
- merge_down: bfloat16 [2560, 4096], P(('tp', 'grp')), may hold values from -0.125 to 0.125
- norm_gain: float32 [4096], replicated, may hold values from 0.1 to 1.9
- query_weight: bfloat16 [4096, 4096], P(None, ('tp', 'grp')), may hold values from -0.62928387 to 0.62928387
- kv_weight: bfloat16 [4096, 2048], P(None, 'tp'), may hold values from -0.4578688 to 0.4578688
Outputs:
- attended: bfloat16 [512, 4096], P('ctx', ('tp', 'grp'))
Inputs may be any that keep to these rules, and one draw needn't show every extreme that they name: route_count[c, d] counts the live rows among the 2 rows that source c holds for owner d; at least one owner gets 2 live rows from every source. `segment_ids`: never falling along the packed batch; a segment has at most 256 positions.
All inputs are finite; a program needn't handle non-finite values.
Results may differ from a plain program's by a relative error of at most 0.04.
Values may be sent and summed in bfloat16 or wider, within the bound.
A program may use at most 64 MiB of HBM per device.

v0:
```python
import jax
import jax.numpy as jnp
from jax import lax
from jax.sharding import PartitionSpec as P

HQ = 32
KVH = 8
HD = 128
EPSILON = 1e-06
NEGATIVE = -1e30


def rms_scale(values, gain):
    mean_square = jnp.mean(values * values, axis=-1, keepdims=True)
    return values * lax.rsqrt(mean_square + EPSILON) * gain


def attend(
    running,
    queries4,
    shard_piece,
    key_pos,
    query_pos,
    query_seg,
    segment_ids,
    visual_count,
    tokens_dev,
):
    weighted, running_max, denominator = running
    piece_rows = shard_piece.shape[0]
    kv_heads = queries4.shape[1]
    kv_split = shard_piece.reshape(piece_rows, kv_heads, 2, HD)
    key_block = kv_split[:, :, 0]
    value_block = kv_split[:, :, 1]
    key_owner = key_pos // tokens_dev
    owner_match = key_owner[:, None] == jnp.arange(visual_count.shape[0], dtype=jnp.int32)[None, :]
    visual_limit = jnp.sum(jnp.where(owner_match, visual_count[None, :], 0), axis=1)
    key_visual = key_pos % tokens_dev < visual_limit
    key_seg = segment_ids[key_pos]
    allowed = (query_seg[:, None] == key_seg[None, :]) & (
        key_visual[None, :] | (key_pos[None, :] <= query_pos[:, None])
    )
    scores = jnp.where(
        allowed,
        jnp.einsum("qkgd,rkd->kgqr", queries4, key_block, preferred_element_type=jnp.float32)
        * HD ** (-0.5),
        NEGATIVE,
    )
    new_max = jnp.maximum(running_max, jnp.max(scores, axis=-1))
    weights = jnp.exp(jnp.where(allowed, scores - new_max[..., None], NEGATIVE))
    denominator = jnp.sum(weights, axis=-1)
    weighted = jnp.einsum(
        "kgqr,rkd->kgqd",
        weights.astype(jnp.bfloat16),
        value_block,
        preferred_element_type=jnp.float32,
    )
    return (weighted, new_max, denominator)


def start_state(kv_heads, per_head, tokens_dev):
    return (
        jnp.zeros((kv_heads, per_head, tokens_dev, HD), jnp.float32),
        jnp.full((kv_heads, per_head, tokens_dev), NEGATIVE, jnp.float32),
        jnp.zeros((kv_heads, per_head, tokens_dev), jnp.float32),
    )


def shards(
    patches,
    route_count,
    text_states,
    segment_ids,
    vision_gain,
    merge_up,
    merge_down,
    norm_gain,
    query_weight,
    kv_weight,
):
    ctx_size = lax.axis_size("ctx")
    grp_size = lax.axis_size("grp")
    tp_size = lax.axis_size("tp")
    owner_index = lax.axis_index("ctx")
    member = lax.axis_index("grp")
    tp_index = lax.axis_index("tp")
    tensor_index = tp_index * grp_size + member
    row_count = patches.shape[0]
    bucket_rows = row_count // ctx_size
    tokens_dev = text_states.shape[0]
    grouped = patches.astype(jnp.float32).reshape(row_count, 4, -1)
    patch_normed = rms_scale(grouped, vision_gain).reshape(row_count, -1).astype(jnp.bfloat16)
    hidden = jax.nn.gelu(
        jnp.dot(patch_normed, merge_up, preferred_element_type=jnp.float32), approximate=False
    ).astype(jnp.bfloat16)
    partial_value = jnp.dot(hidden, merge_down, preferred_element_type=jnp.float32)
    column = lax.dynamic_slice_in_dim(route_count, owner_index, 1, 1)[:, 0]
    count_ends = jnp.cumsum(column)
    count_starts = count_ends - column
    slot_ids = jnp.arange(tokens_dev, dtype=jnp.int32)
    source = jnp.sum((count_ends[None, :] <= slot_ids[:, None]).astype(jnp.int32), axis=1)
    source = jnp.minimum(source, ctx_size - 1)
    source_match = source[:, None] == jnp.arange(ctx_size, dtype=jnp.int32)[None, :]
    first_slot = jnp.sum(jnp.where(source_match, count_starts[None, :], 0), axis=1)
    visual = slot_ids < count_ends[ctx_size - 1]
    pick_rows = jnp.where(visual, source * bucket_rows + slot_ids - first_slot, 0)
    merged = lax.psum(partial_value, ("tp", "grp")).astype(jnp.bfloat16)
    arrived = lax.all_to_all(
        merged.reshape(ctx_size, bucket_rows, -1), "ctx", split_axis=0, concat_axis=0, tiled=True
    )
    arrived = arrived.reshape(row_count, -1)
    text_full = lax.all_gather(text_states, ("tp", "grp"), axis=1, tiled=True)
    packed = jnp.where(visual[:, None], arrived[pick_rows], text_full)
    normal = rms_scale(packed.astype(jnp.float32), norm_gain).astype(jnp.bfloat16)
    queries = jnp.dot(normal, query_weight, preferred_element_type=jnp.float32).astype(jnp.bfloat16)
    kv_pairs = jnp.dot(normal, kv_weight, preferred_element_type=jnp.float32).astype(jnp.bfloat16)
    heads_dev = queries.shape[1] // HD
    group = HQ // KVH
    kv_per_tp = KVH // tp_size
    query_pos = owner_index * tokens_dev + slot_ids
    query_seg = segment_ids[query_pos]
    visual_count = jnp.sum(route_count, axis=0)
    kv_local = tensor_index * heads_dev // group - tp_index * kv_per_tp
    chosen = lax.dynamic_slice_in_dim(kv_pairs, kv_local * 2 * HD, 2 * HD, 1)
    queries4 = queries.reshape(tokens_dev, 1, heads_dev, HD)
    shard_piece = lax.all_gather(chosen, "ctx", axis=0, tiled=True)
    key_pos = jnp.arange(shard_piece.shape[0], dtype=jnp.int32)
    weighted, running_max, denominator = attend(
        start_state(1, heads_dev, tokens_dev),
        queries4,
        shard_piece,
        key_pos,
        query_pos,
        query_seg,
        segment_ids,
        visual_count,
        tokens_dev,
    )
    result = (weighted / denominator[..., None]).reshape(heads_dev, tokens_dev, HD)
    return result.transpose(1, 0, 2).reshape(tokens_dev, -1).astype(jnp.bfloat16)


def solution(mesh):
    return jax.shard_map(
        shards,
        mesh=mesh,
        in_specs=(
            P("ctx", None),
            P(),
            P("ctx", ("tp", "grp")),
            P(),
            P(),
            P(None, ("tp", "grp")),
            P(("tp", "grp"), None),
            P(),
            P(None, ("tp", "grp")),
            P(None, "tp"),
        ),
        out_specs=P("ctx", ("tp", "grp")),
        check_vma=False,
    )
```

profile of v0, /device:TPU:0, one launch (start us, length us, event | category | flops | bytes accessed | tf_op | source)
XLA Modules:
  0.0 106.3 jit_solution(12033060647353405200)
XLA Ops:
  6.5 0.0 copy-start
  6.5 1.0 convert_multiply_fusion.3
  7.6 0.1 reduce_sum.67
  7.7 0.7 mul.112
  8.4 0.1 mul.109
  8.5 0.0 copy-done
  8.5 0.0 copy-start.5
  8.5 0.0 copy-start.1
  8.5 4.6 %fusion.41 = f32[8,4096]{1,0:T(8,128)} fusion(bf16[320,4096]{1,0:T(8,128)(2,1)} %param.16, bf16[5120,320]{0,1:T(8,128)(2,1)S(1)} %copy-done, f32[8,5120]{1,0:T(8,128)S(1)} %bitcast.59, bf16[8,5120]{1,0:T(8,128)(2,1)} %param.10, f32[5120]{0:T(1024)S(1)} %mul.113), kind=kOutput, calls=%fused_computation.58 | convolution fusion | flops 47516160 | bytes 6295552 | tf_op jit(solution)/shard_map/dot_general | solution.py:96
  13.1 32.0 %all-reduce.1 = bf16[8,4096]{1,0:T(8,128)(2,1)S(1)} all-reduce(f32[8,4096]{1,0:T(8,128)} %fusion.41), channel_id=1, replica_groups=mesh['ctx'=4,'tp'=4,'grp'=2] {'tp','grp'}, use_global_device_ids=true, to_apply=%region_4.5 | all-reduce | flops 32768 | bytes 196608 | tf_op jit(solution)/shard_map/psum | solution.py:107
  45.2 0.7 reshape.183
  45.8 3.7 %all-to-all-start = ((bf16[4,2,4096]{2,1,0:T(2,128)(2,1)}), bf16[4,2,4096]{2,1,0:T(2,128)(2,1)S(1)}, u32[]{:S(2)}, u32[]{:S(2)}) async-start(bf16[4,2,4096]{2,1,0:T(2,128)(2,1)} %reshape.183), calls=%async_computation | async-start | bytes 131072 | tf_op jit(solution)/shard_map/all_to_all | solution.py:108
  49.6 0.0 all-gather.2.cloned.1.call-start
  49.6 0.7 all-gather.2.cloned.1.call-update
  50.3 0.0 copy-done.5
  50.3 0.2 fusion.112
  50.6 0.1 reduce.2
  50.7 0.6 slice.10
  51.3 0.0 copy-done.1
  51.3 1.3 %gather_fusion = s32[128]{0:T(128)S(1)} fusion(s32[512]{0:T(512)S(1)} %copy-done.1, s32[1024]{0:T(1024)S(1)} %pad_clamp_fusion.1), kind=kCustom, calls=%fused_computation | custom fusion | bytes 1536 | tf_op jit(solution)/shard_map/gather | solution.py:121
  52.6 3.5 %gather_fusion.1 = s32[512]{0:T(512)S(1)} fusion(s32[512]{0:T(512)S(1)} %copy-done.1, s32[1024]{0:T(1024)S(1)} %pad_clamp_fusion), kind=kCustom, calls=%fused_computation.1 | custom fusion | bytes 6144 | tf_op jit(solution)/shard_map/gather | solution.py:39
  56.1 0.1 convert_reduce_fusion
  56.2 0.1 select_reduce_fusion.1
  56.3 0.7 fusion.80
  57.0 0.1 select_reduce_fusion
  57.1 0.8 fusion.19
  57.9 0.7 iota_compare_fusion.4
  58.7 0.0 all-to-all-done
  58.7 2.2 %gather_fusion.2 = bf16[128,4096]{1,0:T(8,128)(2,1)} fusion(bf16[8,4096]{1,0:T(8,128)(2,1)S(1)} %reshape.184, s32[1024]{0:T(1024)S(1)} %pad_clamp_fusion.2), kind=kCustom, calls=%fused_computation.2 | custom fusion | bytes 2097664 | tf_op jit(solution)/shard_map/gather | solution.py:113
  60.9 12.1 %all-gather.2.cloned.1.call-done = bf16[128,4096]{1,0:T(8,128)(2,1)} async-done(((bf16[128,512]{1,0:T(8,128)(2,1)}), bf16[128,4096]{1,0:T(8,128)(2,1)}) %all-gather.2.cloned.1.call-update) | async-done | bytes 1048592 | tf_op jit(solution)/shard_map/all_gather | solution.py:112
  73.0 2.2 %fusion = (f32[128]{0:T(128)S(1)}, bf16[128,4096]{1,0:T(8,128)(2,1)S(1)}) fusion(bf16[128,4096]{1,0:T(8,128)(2,1)} %gather_fusion.2, bf16[128,4096]{1,0:T(8,128)(2,1)} %all-gather.2.cloned.1.call-done, pred[128]{0:T(512)(128)(4,1)S(1)} %iota_compare_fusion.4), kind=kLoop, calls=%fused_computation.5 | loop fusion | flops 2097024 | bytes 3146368 | tf_op jit(solution)/shard_map/reduce_sum | solution.py:14
  75.2 0.0 copy-start.2
  75.2 0.0 copy-start.7
  75.2 0.0 copy-done.6
  75.2 3.3 %fusion.16 = bf16[128,512]{1,0:T(8,128)(2,1)S(1)} fusion(bf16[4096,512]{1,0:T(8,128)(2,1)} %param.19, bf16[128,4096]{1,0:T(8,128)(2,1)S(1)} %get-tuple-element.6, f32[4096]{0:T(1024)S(1)} %copy-done.6, f32[128]{0:T(128)S(1)} %add_rsqrt_fusion.1), kind=kOutput, calls=%fused_computation.24 | convolution fusion | flops 538968064 | bytes 5390848 | tf_op jit(solution)/shard_map/dot_general | solution.py:116
  78.6 0.0 copy-done.2
  78.6 0.0 copy-done.7
  78.6 9.6 %all_gather.7 = bf16[512,256]{1,0:T(8,128)(2,1)} all-gather(bf16[128,256]{1,0:T(8,128)(2,1)S(1)} %dynamic-slice_convert_fusion), channel_id=1, replica_groups=mesh['ctx'=4,'tp'=4,'grp'=2] {'ctx'}, dimensions={0}, use_global_device_ids=true | all-gather | bytes 327680 | tf_op jit(solution)/shard_map/all_gather | solution.py:126
  88.2 1.0 reshape.185
  89.2 1.1 %fusion.113 = (bf16[512,1,1,128]{3,2,0,1:T(2,128)(2,1)}, bf16[512,1,1,128]{3,2,0,1:T(2,128)(2,1)S(1)}) fusion(bf16[512,1,2,128]{3,2,0,1:T(2,128)(2,1)S(1)} %reshape.185), kind=kLoop, calls=%fused_computation.155 | loop fusion | bytes 524288 | tf_op jit(solution)/shard_map/slice | solution.py:34
  90.3 3.3 %fusion.7 = bf16[16,4,8,128]{3,2,1,0:T(8,128)(2,1)S(1)} fusion(bf16[4096,512]{1,0:T(8,128)(2,1)} %param.18, bf16[128,4096]{1,0:T(8,128)(2,1)} %copy-done.2, f32[4096]{0:T(1024)S(1)} %copy-done.6, f32[128]{0:T(128)} %copy-done.7), kind=kOutput, calls=%fused_computation.15 | convolution fusion | flops 539033600 | bytes 5390848 | tf_op jit(solution)/shard_map/dot_general | solution.py:115
  93.6 0.0 copy-done.4
  93.6 1.3 %fusion.114 = (f32[4,128]{1,0:T(4,128)S(1)}, f32[1,4,128,512]{2,3,1,0:T(8,128)}) fusion(bf16[16,4,8,128]{3,2,1,0:T(8,128)(2,1)S(1)} %fusion.7, bf16[512,1,1,128]{3,2,0,1:T(2,128)(2,1)S(1)} %get-tuple-element.10, pred[128,512]{0,1:T(8,128)(4,1)S(1)} %copy-done.4), kind=kOutput, calls=%fused_computation.156 | convolution fusion | flops 67894784 | bytes 1378304 | tf_op jit(solution)/shard_map/qkgd,rkd->kgqr/dot_general | solution.py:45
  94.9 0.0 copy-done.3
  94.9 0.8 copy.27
  95.7 1.4 %fusion.8 = f32[4,128]{1,0:T(4,128)S(1)} fusion(f32[1,4,128,512]{2,3,1,0:T(8,128)} %get-tuple-element.12, f32[4,128]{1,0:T(4,128)S(1)} %broadcast_maximum_fusion, pred[128,512]{0,1:T(8,128)(4,1)} %fusion.19), kind=kLoop, calls=%fused_computation.18 | loop fusion | flops 785920 | bytes 1118208 | tf_op jit(solution)/shard_map/reduce_sum | solution.py:51
  97.1 1.6 %fusion.6 = bf16[128,4,128]{0,2,1:T(8,128)(2,1)S(1)} fusion(f32[1,4,128,512]{2,3,1,0:T(8,128)} %get-tuple-element.12, f32[4,128]{1,0:T(4,128)S(1)} %broadcast_maximum_fusion, pred[128,512]{0,1:T(8,128)(4,1)} %fusion.19, bf16[512,1,1,128]{0,3,2,1:T(8,128)(2,1)} %copy.27, f32[128,4]{0,1:T(4,128)S(1)} %bitcast.62), kind=kOutput, calls=%fused_computation.13 | convolution fusion | flops 68026368 | bytes 1380352 | tf_op jit(solution)/shard_map/kgqr,rkd->kgqd/dot_general | solution.py:52
  98.7 0.8 copy.25
  (21 shorter events, 0.2 us)
Async XLA Ops:
  6.5 2.0 %copy-start = (bf16[5120,320]{0,1:T(8,128)(2,1)S(1)}, bf16[5120,320]{0,1:T(8,128)(2,1)}, u32[]{:S(2)}) copy-start(bf16[5120,320]{0,1:T(8,128)(2,1)} %param.15) | copy-start | bytes 9830404
  8.5 41.8 %copy-start.5 = (s32[4,4]{1,0:T(4,128)S(1)}, s32[4,4]{1,0:T(4,128)}, u32[]{:S(2)}) copy-start(s32[4,4]{1,0:T(4,128)} %param.11) | copy-start | bytes 196
  8.5 42.8 %copy-start.1 = (s32[512]{0:T(512)S(1)}, s32[512]{0:T(512)}, u32[]{:S(2)}) copy-start(s32[512]{0:T(512)} %param.13) | copy-start | bytes 6148
  45.8 12.8 %all-to-all-start = ((bf16[4,2,4096]{2,1,0:T(2,128)(2,1)}), bf16[4,2,4096]{2,1,0:T(2,128)(2,1)S(1)}, u32[]{:S(2)}, u32[]{:S(2)}) async-start(bf16[4,2,4096]{2,1,0:T(2,128)(2,1)} %reshape.183), calls=%async_computation | async-start | bytes 131072 | tf_op jit(solution)/shard_map/all_to_all | solution.py:108
  49.6 23.5 %all-gather.2.cloned.1.call-start = ((), (), s32[]{:S(2)}) async-start(), calls=%async_computation.1 | async-start | bytes 1179648 | tf_op jit(solution)/shard_map/all_gather | solution.py:112
  60.9 14.3 %copy-start.6 = (f32[4096]{0:T(1024)S(1)}, f32[4096]{0:T(1024)}, u32[]{:S(2)}) copy-start(f32[4096]{0:T(1024)} %param.17) | copy-start | bytes 49156
  75.2 3.4 %copy-start.2 = (bf16[128,4096]{1,0:T(8,128)(2,1)}, bf16[128,4096]{1,0:T(8,128)(2,1)S(1)}, u32[]{:S(2)}) copy-start(bf16[128,4096]{1,0:T(8,128)(2,1)S(1)} %get-tuple-element.6) | copy-start | bytes 3145732
  75.2 3.4 %copy-start.7 = (f32[128]{0:T(128)}, f32[128]{0:T(128)S(1)}, u32[]{:S(2)}) copy-start(f32[128]{0:T(128)S(1)} %add_rsqrt_fusion.1) | copy-start | bytes 1540
  90.3 3.3 %copy-start.4 = (pred[128,512]{0,1:T(8,128)(4,1)S(1)}, pred[128,512]{0,1:T(8,128)(4,1)}, u32[]{:S(2)}) copy-start(pred[128,512]{0,1:T(8,128)(4,1)} %fusion.19) | copy-start | bytes 196612
  90.3 4.6 %copy-start.3 = (bf16[512,1,1,128]{3,2,0,1:T(2,128)(2,1)S(1)}, bf16[512,1,1,128]{3,2,0,1:T(2,128)(2,1)}, u32[]{:S(2)}) copy-start(bf16[512,1,1,128]{3,2,0,1:T(2,128)(2,1)} %get-tuple-element.9) | copy-start | bytes 393220
Sparse Core Ops, SparseCore 0:
  52.0 21.0 all-gather.1
where the time goes:
time: 107 us; the launch traced here: 106 us
  blocking collectives  41.6 us (39%)
  matrix products  14.1 us (13%)
  between operations  13.7 us (13%)
  local copies, waits for them, and re-layouts  13 us (12%)
  waiting for transfers between devices  12.8 us (12%)
  other arithmetic  7.46 us (7%)
  starting transfers between devices  3.72 us (3%)
    psum x1, blocking collectives, shards(): merged = lax.psum(partial_value, ('tp', 'grp')).astype(jnp.bfloat16)  32 us
    all_gather x1, waiting for transfers between devices, shards(): text_full = lax.all_gather(text_states, ('tp', 'grp'), axis=1, tiled=True)  12.1 us
    all_gather x1, blocking collectives, shards(): shard_piece = lax.all_gather(chosen, 'ctx', axis=0, tiled=True)  9.55 us
    dot_general x1, matrix products, shards(): jnp.dot(hidden, merge_down, preferred_element_type=jnp.float32)  4.57 us
    all_to_all x1, starting transfers between devices, shards(): lax.all_to_all(merged.reshape(ctx_size, bucket_rows, -1), 'ctx', split_ax...  3.72 us
    gather x1, local copies, waits for them, and re-layouts, attend(): key_seg = segment_ids[key_pos]  3.49 us
    dot_general x1, matrix products, shards(): jnp.dot(normal, kv_weight, preferred_element_type=jnp.float32)  3.34 us
    dot_general x1, matrix products, shards(): jnp.dot(normal, query_weight, preferred_element_type=jnp.float32)  3.32 us
  transfers between devices with their start and end apart: 2, of which 1 were waited for; matrix products, arithmetic and copies ran while one was open for 10% of the time, Pallas kernels for 0%

commit v1 on v0

--- a/solution.py
+++ b/solution.py
@@ -123,7 +123,12 @@
     kv_local = tensor_index * heads_dev // group - tp_index * kv_per_tp
     chosen = lax.dynamic_slice_in_dim(kv_pairs, kv_local * 2 * HD, 2 * HD, 1)
     queries4 = queries.reshape(tokens_dev, 1, heads_dev, HD)
-    shard_piece = lax.all_gather(chosen, "ctx", axis=0, tiled=True)
+    ring = [chosen]
+    for hop in range(3):
+        ring.append(lax.ppermute(ring[-1], "ctx", [(dev, (dev + 1) % 4) for dev in range(4)]))
+    shard_piece = jnp.roll(
+        jnp.concatenate(ring[::-1], axis=0), (lax.axis_index("ctx") + 1) * ring[0].shape[0], axis=0
+    )
     key_pos = jnp.arange(shard_piece.shape[0], dtype=jnp.int32)
     weighted, running_max, denominator = attend(
         start_state(1, heads_dev, tokens_dev),

time: 107 us -> 95.1 us (0.89)
  blocking collectives: 41.6 us -> 33.1 us
  waiting for transfers between devices: 12.8 us -> 8.07 us
  starting transfers between devices: 3.72 us -> 7.08 us
  local copies, waits for them, and re-layouts: 13 us -> 11 us
    all_gather x1, waiting for transfers between devices: 12.1 us -> 0.01 us  [shards(): text_full = lax.all_gather(text_states, ('tp', 'grp'), axis=1, tiled=True)]
    all_gather x1 -> x0, blocking collectives: 9.55 us -> none  [shards(): shard_piece = lax.all_gather(chosen, 'ctx', axis=0, tiled=True)]
    ppermute x0 -> x3, waiting for transfers between devices: none -> 7.35 us  [shards(): lax.ppermute(ring[-1], 'ctx', [(dev, (dev + 1) % 4) for dev in range(4)])]
    ppermute x0 -> x3, starting transfers between devices: none -> 3.42 us  [shards(): lax.ppermute(ring[-1], 'ctx', [(dev, (dev + 1) % 4) for dev in range(4)])]
    slice x1 -> x0, local copies, waits for them, and re-layouts: 1.08 us -> none  [attend(): value_block = kv_split[:, :, 1]]
  transfers between devices with their start and end apart: 2 -> 5, of which waited for: 1 -> 3; matrix products, arithmetic and copies ran while one was open for 10% -> 23% of each run, Pallas kernels for 0% -> 0%
where the time goes in v1:
time: 95.1 us; the launch traced here: 94.6 us
  blocking collectives  33.1 us (35%)
  matrix products  14.4 us (15%)
  between operations  13.7 us (14%)
  local copies, waits for them, and re-layouts  11 us (12%)
  waiting for transfers between devices  8.07 us (8%)
  other arithmetic  7.19 us (8%)
  starting transfers between devices  7.08 us (7%)
    psum x1, blocking collectives, shards(): merged = lax.psum(partial_value, ('tp', 'grp')).astype(jnp.bfloat16)  33.1 us
    ppermute x3, waiting for transfers between devices, shards(): lax.ppermute(ring[-1], 'ctx', [(dev, (dev + 1) % 4) for dev in range(4)])  7.35 us
    dot_general x1, matrix products, shards(): jnp.dot(hidden, merge_down, preferred_element_type=jnp.float32)  4.57 us
    dot_general x1, matrix products, shards(): jnp.dot(normal, query_weight, preferred_element_type=jnp.float32)  3.95 us
    all_to_all x1, starting transfers between devices, shards(): lax.all_to_all(merged.reshape(ctx_size, bucket_rows, -1), 'ctx', split_ax...  3.65 us
    gather x1, local copies, waits for them, and re-layouts, attend(): key_seg = segment_ids[key_pos]  3.49 us
    ppermute x3, starting transfers between devices, shards(): lax.ppermute(ring[-1], 'ctx', [(dev, (dev + 1) % 4) for dev in range(4)])  3.42 us
    dot_general x1, matrix products, shards(): jnp.dot(normal, kv_weight, preferred_element_type=jnp.float32)  3.37 us
  transfers between devices with their start and end apart: 5, of which 3 were waited for; matrix products, arithmetic and copies ran while one was open for 23% of the time, Pallas kernels for 0%

profile of v1, /device:TPU:0, one launch (start us, length us, event | category | flops | bytes accessed | tf_op | source)
XLA Modules:
  0.0 94.6 jit_solution(17619007170367978745)
XLA Ops:
  6.5 0.0 copy-start
  6.5 0.0 all-gather.2.cloned.1.call-start
  6.5 0.7 all-gather.2.cloned.1.call-update
  7.3 1.2 %convert_multiply_fusion.3 = f32[8,5120]{1,0:T(8,128)S(1)} fusion(bf16[8,5120]{1,0:T(8,128)(2,1)} %param.10), kind=kLoop, calls=%fused_computation.29 | loop fusion | flops 81920 | bytes 245760 | tf_op jit(solution)/shard_map/mul | solution.py:14
  8.4 0.1 reduce_sum.67
  8.5 0.7 mul.115
  9.3 0.1 mul.112
  9.3 0.0 copy-done
  9.3 0.0 copy-start.3
  9.4 0.0 copy-start.1
  9.4 4.6 %fusion.40 = f32[8,4096]{1,0:T(8,128)} fusion(bf16[320,4096]{1,0:T(8,128)(2,1)} %param.16, bf16[5120,320]{0,1:T(8,128)(2,1)S(1)} %copy-done, f32[8,5120]{1,0:T(8,128)S(1)} %bitcast.61, bf16[8,5120]{1,0:T(8,128)(2,1)} %param.10, f32[5120]{0:T(1024)S(1)} %mul.116), kind=kOutput, calls=%fused_computation.66 | convolution fusion | flops 47516160 | bytes 6295552 | tf_op jit(solution)/shard_map/dot_general | solution.py:96
  13.9 33.1 %all-reduce.1 = bf16[8,4096]{1,0:T(8,128)(2,1)S(1)} all-reduce(f32[8,4096]{1,0:T(8,128)} %fusion.40), channel_id=1, replica_groups=mesh['ctx'=4,'tp'=4,'grp'=2] {'tp','grp'}, use_global_device_ids=true, to_apply=%region_4.5 | all-reduce | flops 32768 | bytes 196608 | tf_op jit(solution)/shard_map/psum | solution.py:107
  47.0 0.7 reshape.183
  47.7 3.7 %all-to-all-start = ((bf16[4,2,4096]{2,1,0:T(2,128)(2,1)}), bf16[4,2,4096]{2,1,0:T(2,128)(2,1)S(1)}, u32[]{:S(2)}, u32[]{:S(2)}) async-start(bf16[4,2,4096]{2,1,0:T(2,128)(2,1)} %reshape.183), calls=%async_computation | async-start | bytes 131072 | tf_op jit(solution)/shard_map/all_to_all | solution.py:108
  51.4 0.0 copy-done.3
  51.4 0.2 fusion.111
  51.6 0.1 reduce.2
  51.7 0.6 slice.10
  52.4 0.1 convert_reduce_fusion
  52.5 0.1 select_reduce_fusion.1
  52.5 0.7 fusion.79
  53.3 0.1 select_reduce_fusion
  53.4 0.7 iota_compare_fusion.4
  54.1 0.0 copy-done.1
  54.1 1.3 %gather_fusion = s32[128]{0:T(128)S(1)} fusion(s32[512]{0:T(512)S(1)} %copy-done.1, s32[1024]{0:T(1024)S(1)} %pad_clamp_fusion.1), kind=kCustom, calls=%fused_computation | custom fusion | bytes 1536 | tf_op jit(solution)/shard_map/gather | solution.py:121
  55.4 3.5 %gather_fusion.1 = s32[512]{0:T(512)S(1)} fusion(s32[512]{0:T(512)S(1)} %copy-done.1, s32[1024]{0:T(1024)S(1)} %pad_clamp_fusion), kind=kCustom, calls=%fused_computation.1 | custom fusion | bytes 6144 | tf_op jit(solution)/shard_map/gather | solution.py:39
  58.9 0.0 all-to-all-done
  58.9 2.2 %gather_fusion.2 = bf16[128,4096]{1,0:T(8,128)(2,1)} fusion(bf16[8,4096]{1,0:T(8,128)(2,1)S(1)} %reshape.184, s32[1024]{0:T(1024)S(1)} %pad_clamp_fusion.2), kind=kCustom, calls=%fused_computation.2 | custom fusion | bytes 2097664 | tf_op jit(solution)/shard_map/gather | solution.py:113
  61.2 0.0 copy-start.4
  61.2 0.0 all-gather.2.cloned.1.call-done
  61.2 2.2 %fusion = (f32[128]{0:T(128)S(1)}, bf16[128,4096]{1,0:T(8,128)(2,1)S(1)}) fusion(bf16[128,4096]{1,0:T(8,128)(2,1)} %gather_fusion.2, bf16[128,4096]{1,0:T(8,128)(2,1)} %all-gather.2.cloned.1.call-done, pred[128]{0:T(512)(128)(4,1)S(1)} %iota_compare_fusion.4), kind=kLoop, calls=%fused_computation.5 | loop fusion | flops 2097024 | bytes 3146368 | tf_op jit(solution)/shard_map/reduce_sum | solution.py:14
  63.3 0.0 copy-start.2
  63.4 0.0 copy-done.4
  63.4 3.4 %fusion.16 = bf16[128,512]{1,0:T(8,128)(2,1)S(1)} fusion(bf16[4096,512]{1,0:T(8,128)(2,1)} %param.19, bf16[128,4096]{1,0:T(8,128)(2,1)S(1)} %get-tuple-element.6, f32[4096]{0:T(1024)S(1)} %copy-done.4, f32[128]{0:T(128)S(1)} %add_rsqrt_fusion.1), kind=kOutput, calls=%fused_computation.24 | convolution fusion | flops 538968064 | bytes 5390848 | tf_op jit(solution)/shard_map/dot_general | solution.py:116
  66.8 0.0 copy-done.2
  66.8 2.1 %collective-permute-start = (bf16[128,256]{1,0:T(8,128)(2,1)S(1)}, bf16[128,256]{1,0:T(8,128)(2,1)S(1)}, u32[]{:S(2)}, u32[]{:S(2)}) collective-permute-start(bf16[128,256]{1,0:T(8,128)(2,1)S(1)} %dynamic-slice_convert_fusion), channel_id=1, source_target_pairs={{0,8},{8,16},{16,24},{24,0},{1,9},{9,17},{17,25},{25,1},{2,10},{10... | collective-permute-start | bytes 196616 | tf_op jit(solution)/shard_map/ppermute | solution.py:128
  68.9 3.1 %collective-permute-done = bf16[128,256]{1,0:T(8,128)(2,1)S(1)} collective-permute-done((bf16[128,256]{1,0:T(8,128)(2,1)S(1)}, bf16[128,256]{1,0:T(8,128)(2,1)S(1)}, u32[]{:S(2)}, u32[]{:S(2)}) %collective-permute-start) | collective-permute-done | bytes 65568 | tf_op jit(solution)/shard_map/ppermute | solution.py:128
  72.0 1.1 %collective-permute-start.1 = (bf16[128,256]{1,0:T(8,128)(2,1)S(1)}, bf16[128,256]{1,0:T(8,128)(2,1)S(1)}, u32[]{:S(2)}, u32[]{:S(2)}) collective-permute-start(bf16[128,256]{1,0:T(8,128)(2,1)S(1)} %collective-permute-done), channel_id=1, source_target_pairs={{0,8},{8,16},{16,24},{24,0},{1,9},{9,17},{17,25},{25,1},{2,10},{10... | collective-permute-start | bytes 196616 | tf_op jit(solution)/shard_map/ppermute | solution.py:128
  73.1 0.8 fusion.19
  74.0 3.2 %collective-permute-done.1 = bf16[128,256]{1,0:T(8,128)(2,1)S(1)} collective-permute-done((bf16[128,256]{1,0:T(8,128)(2,1)S(1)}, bf16[128,256]{1,0:T(8,128)(2,1)S(1)}, u32[]{:S(2)}, u32[]{:S(2)}) %collective-permute-start.1) | collective-permute-done | bytes 65568 | tf_op jit(solution)/shard_map/ppermute | solution.py:128
  77.2 0.2 collective-permute-start.2
  77.4 3.9 %fusion.7 = bf16[16,4,8,128]{3,2,1,0:T(8,128)(2,1)} fusion(bf16[4096,512]{1,0:T(8,128)(2,1)} %param.18, bf16[128,4096]{1,0:T(8,128)(2,1)} %copy-done.2, f32[4096]{0:T(1024)} %param.17, f32[128]{0:T(128)S(1)} %add_rsqrt_fusion.1), kind=kOutput, calls=%fused_computation.15 | convolution fusion | flops 539033600 | bytes 5390848 | tf_op jit(solution)/shard_map/dot_general | solution.py:115
  81.3 1.0 %collective-permute-done.2 = bf16[128,256]{1,0:T(8,128)(2,1)S(1)} collective-permute-done((bf16[128,256]{1,0:T(8,128)(2,1)S(1)}, bf16[128,256]{1,0:T(8,128)(2,1)S(1)}, u32[]{:S(2)}, u32[]{:S(2)}) %collective-permute-start.2) | collective-permute-done | bytes 65568 | tf_op jit(solution)/shard_map/ppermute | solution.py:128
  82.5 0.8 copy.20
  83.3 1.3 %fusion.112 = (f32[4,128]{1,0:T(4,128)S(1)}, f32[1,4,128,512]{2,3,1,0:T(8,128)S(1)}) fusion(bf16[16,4,8,128]{3,2,1,0:T(8,128)(2,1)} %fusion.7, bf16[512,1,2,128]{0,3,2,1:T(8,128)(2,1)} %bitcast.63, pred[128,512]{0,1:T(8,128)(4,1)} %fusion.19), kind=kOutput, calls=%fused_computation.164 | convolution fusion | flops 67894784 | bytes 1378304 | tf_op jit(solution)/shard_map/qkgd,rkd->kgqr/dot_general | solution.py:45
  84.6 1.0 %fusion.8 = f32[4,128]{1,0:T(4,128)S(1)} fusion(f32[1,4,128,512]{2,3,1,0:T(8,128)S(1)} %get-tuple-element.10, f32[4,128]{1,0:T(4,128)S(1)} %broadcast_maximum_fusion, pred[128,512]{0,1:T(8,128)(4,1)} %fusion.19), kind=kLoop, calls=%fused_computation.18 | loop fusion | flops 785920 | bytes 1118208 | tf_op jit(solution)/shard_map/reduce_sum | solution.py:51
  85.7 1.3 %fusion.6 = bf16[128,4,128]{0,2,1:T(8,128)(2,1)S(1)} fusion(f32[1,4,128,512]{2,3,1,0:T(8,128)S(1)} %get-tuple-element.10, f32[4,128]{1,0:T(4,128)S(1)} %broadcast_maximum_fusion, pred[128,512]{0,1:T(8,128)(4,1)} %fusion.19, bf16[512,1,2,128]{0,3,2,1:T(8,128)(2,1)} %bitcast.64, f32[128,4]{0,1:T(4,128)S(1)} %bitcast.66), kind=kOutput, calls=%fused_computation.13 | convolution fusion | flops 68026368 | bytes 1380352 | tf_op jit(solution)/shard_map/kgqr,rkd->kgqd/dot_general | solution.py:52
  87.0 0.8 copy.24
  (27 shorter events, 0.3 us)
Async XLA Ops:
  6.5 2.8 %copy-start = (bf16[5120,320]{0,1:T(8,128)(2,1)S(1)}, bf16[5120,320]{0,1:T(8,128)(2,1)}, u32[]{:S(2)}) copy-start(bf16[5120,320]{0,1:T(8,128)(2,1)} %param.15) | copy-start | bytes 9830404
  6.5 54.6 %all-gather.2.cloned.1.call-start = ((), (), s32[]{:S(2)}) async-start(), calls=%async_computation.1 | async-start | bytes 1179648 | tf_op jit(solution)/shard_map/all_gather | solution.py:112
  9.3 42.0 %copy-start.3 = (s32[4,4]{1,0:T(4,128)S(1)}, s32[4,4]{1,0:T(4,128)}, u32[]{:S(2)}) copy-start(s32[4,4]{1,0:T(4,128)} %param.11) | copy-start | bytes 196
  9.4 44.8 %copy-start.1 = (s32[512]{0:T(512)S(1)}, s32[512]{0:T(512)}, u32[]{:S(2)}) copy-start(s32[512]{0:T(512)} %param.13) | copy-start | bytes 6148
  47.7 11.2 %all-to-all-start = ((bf16[4,2,4096]{2,1,0:T(2,128)(2,1)}), bf16[4,2,4096]{2,1,0:T(2,128)(2,1)S(1)}, u32[]{:S(2)}, u32[]{:S(2)}) async-start(bf16[4,2,4096]{2,1,0:T(2,128)(2,1)} %reshape.183), calls=%async_computation | async-start | bytes 131072 | tf_op jit(solution)/shard_map/all_to_all | solution.py:108
  61.2 2.2 %copy-start.4 = (f32[4096]{0:T(1024)S(1)}, f32[4096]{0:T(1024)}, u32[]{:S(2)}) copy-start(f32[4096]{0:T(1024)} %param.17) | copy-start | bytes 49156
  63.3 3.4 %copy-start.2 = (bf16[128,4096]{1,0:T(8,128)(2,1)}, bf16[128,4096]{1,0:T(8,128)(2,1)S(1)}, u32[]{:S(2)}) copy-start(bf16[128,4096]{1,0:T(8,128)(2,1)S(1)} %get-tuple-element.6) | copy-start | bytes 3145732
  66.8 5.2 %collective-permute-start = (bf16[128,256]{1,0:T(8,128)(2,1)S(1)}, bf16[128,256]{1,0:T(8,128)(2,1)S(1)}, u32[]{:S(2)}, u32[]{:S(2)}) collective-permute-start(bf16[128,256]{1,0:T(8,128)(2,1)S(1)} %dynamic-slice_convert_fusion), channel_id=1, source_target_pairs={{0,8},{8,16},{16,24},{24,0},{1,9},{9,17},{17,25},{25,1},{2,10},{10... | collective-permute-start | bytes 196616 | tf_op jit(solution)/shard_map/ppermute | solution.py:128
  72.0 5.2 %collective-permute-start.1 = (bf16[128,256]{1,0:T(8,128)(2,1)S(1)}, bf16[128,256]{1,0:T(8,128)(2,1)S(1)}, u32[]{:S(2)}, u32[]{:S(2)}) collective-permute-start(bf16[128,256]{1,0:T(8,128)(2,1)S(1)} %collective-permute-done), channel_id=1, source_target_pairs={{0,8},{8,16},{16,24},{24,0},{1,9},{9,17},{17,25},{25,1},{2,10},{10... | collective-permute-start | bytes 196616 | tf_op jit(solution)/shard_map/ppermute | solution.py:128
  77.2 5.2 %collective-permute-start.2 = (bf16[128,256]{1,0:T(8,128)(2,1)S(1)}, bf16[128,256]{1,0:T(8,128)(2,1)S(1)}, u32[]{:S(2)}, u32[]{:S(2)}) collective-permute-start(bf16[128,256]{1,0:T(8,128)(2,1)S(1)} %collective-permute-done.1), channel_id=1, source_target_pairs={{0,8},{8,16},{16,24},{24,0},{1,9},{9,17},{17,25},{25,1},{2,10},{10... | collective-permute-start | bytes 196616 | tf_op jit(solution)/shard_map/ppermute | solution.py:128
Sparse Core Ops, SparseCore 0:
  8.9 25.5 all-gather.1
